TPU v7x, 32 devices: a whole 2x2x4 slice. The times are simulated.
32 devices in a mesh: box: 8 (over z, y), nbr: 4 (over x, core).
Axes of the slice: x: 2, y: 2, z: 4, core: 2. Of those that a mesh axis runs over, the one named last changes fastest.
Arguments:
- self_block: float32 [64, 256, 256], P('box', 'nbr'), as said below
- ordering: int32 [64, 256], P('box'), may hold values from 0 to 255, each once within a row
- interp: float32 [64, 64, 192], P('box'), may hold values from -0.12 to 0.12
- near_band: float32 [64, 8, 2, 64, 256], P('box', 'nbr'), may hold values from -3 to 3
- pair_mask: int32 [64, 8], P('box', 'nbr'), may hold values 0 or 1
Outputs:
- skeleton_self: float32 [64, 64, 64], P('box')
- red_inverse: float32 [64, 192, 192], P('box', 'nbr')
- couplings: float32 [64, 8, 64, 128], P('box', 'nbr')
Inputs may be any that keep to these rules, and one draw needn't show every extreme that they name: Each row of ordering is a permutation of the 256 unknowns of its box. Each self_block[b] has a positive diagonal.
All inputs are finite; a program needn't handle non-finite values. No bound on the sum of `pair_mask` on one device may be relied on, other than what follows from the above.
Results may differ from a plain program's by a relative error of at most 0.0003.
Values sent between devices are 32-bit elements; how exact they have to be, the bound alone decides.
A program may use at most 128 MiB of HBM per device.

v0:
```python
import jax
import jax.numpy as jnp
from jax import lax
from jax.sharding import PartitionSpec as P

SKEL = 64
RED = 192
REACH = 4
NS_ITERS = 3


def extended_2(block, sides, width):
    for axis, dim in sides:
        count = lax.axis_size(axis)
        forward = [(i, i + 1) for i in range(count - 1)]
        forward.append((count - 1, 0))
        backward = [(target, source) for source, target in forward]
        low = lax.ppermute(
            lax.slice_in_dim(block, block.shape[dim] - width, None, axis=dim), axis, forward
        )
        high = lax.ppermute(lax.slice_in_dim(block, 0, width, axis=dim), axis, backward)
        block = jnp.concatenate([low, block, high], axis=dim)
    return block


def passed_along(block, axis, distance):
    devices = range(lax.axis_size(axis))
    route = [((i - distance) % len(devices), i) for i in devices]
    return lax.ppermute(block, axis, route)


def product(pattern, left_term, right_term):
    return jnp.einsum(pattern, left_term, right_term, precision=lax.Precision.HIGHEST)


def selector(ordering):
    columns = jnp.arange(ordering.shape[1], dtype=jnp.int32)
    return (ordering[:, :, None] == columns[None, None, :]).astype(jnp.float32)


def permuted(matrix, chooser):
    row_sorted = product("bik,bkj->bij", chooser, matrix)
    return product("bik,bjk->bij", row_sorted, chooser)


def factors(matrix, chooser, interp):
    full_block = permuted(matrix, chooser)
    skel_skel = full_block[:, :SKEL, :SKEL]
    skel_red = full_block[:, :SKEL, SKEL:]
    red_skel = full_block[:, SKEL:, :SKEL]
    red_red = full_block[:, SKEL:, SKEL:]
    skel_interp = product("bij,bjk->bik", skel_skel, interp)
    x_skel_red = skel_red - skel_interp
    x_red_skel = red_skel - product("bji,bjk->bik", interp, skel_skel)
    x_red_red = (
        red_red
        - product("bji,bjk->bik", interp, skel_red)
        - product("bij,bjk->bik", red_skel, interp)
    )
    x_red_red = x_red_red + product("bji,bjk->bik", interp, skel_interp)
    identity = jnp.eye(RED, dtype=jnp.float32)
    diag_vals = jnp.diagonal(red_red, axis1=1, axis2=2)
    approx = identity[None] / diag_vals[:, None, :]
    for sweep_index in range(NS_ITERS):
        approx = 2.0 * approx - product(
            "bij,bjk->bik", approx, product("bij,bjk->bik", x_red_red, approx)
        )
    left_factor = product("bij,bjk->bik", x_skel_red, approx)
    right_factor = product("bij,bjk->bik", approx, x_red_skel)
    own_block = skel_skel - product("bij,bjk->bik", left_factor, x_red_skel)
    return (approx, left_factor, right_factor, own_block)


def slot_terms(near_piece, chooser, interp, approx, left_factor, right_factor):
    both_parts = product("bpik,bjk->bpij", near_piece, chooser)
    row_part = both_parts[:, 0]
    col_part = both_parts[:, 1]
    near_red = row_part[:, :, SKEL:] - product("bij,bjk->bik", row_part[:, :, :SKEL], interp)
    red_near_t = col_part[:, :, SKEL:] - product("bij,bjk->bik", col_part[:, :, :SKEL], interp)
    new_forward = jnp.swapaxes(col_part[:, :, :SKEL], 1, 2) - product(
        "bij,bkj->bik", left_factor, red_near_t
    )
    new_backward = jnp.swapaxes(row_part[:, :, :SKEL], 1, 2) - product(
        "bji,bkj->bik", right_factor, near_red
    )
    coupled = jnp.concatenate([new_forward, new_backward], axis=2)
    update = product("bij,bkj->bik", product("bij,bjk->bik", near_red, approx), red_near_t)
    return (coupled, update)


def body(self_block, ordering, interp, near_band, pair_mask):
    box_count = ordering.shape[0]
    nbr_count = lax.axis_size("nbr")
    nbr_place = lax.axis_index("nbr")
    chooser = selector(ordering)
    share_boxes = box_count // nbr_count
    own_rows = lax.all_to_all(self_block, "nbr", split_axis=0, concat_axis=1, tiled=True)
    my_chooser = lax.dynamic_slice_in_dim(chooser, nbr_place * share_boxes, share_boxes, 0)
    my_interp = lax.dynamic_slice_in_dim(interp, nbr_place * share_boxes, share_boxes, 0)
    part_inverse, part_left, part_right, part_own = factors(own_rows, my_chooser, my_interp)
    approx, left_factor, right_factor, own_block = (
        lax.all_gather(part_inverse, "nbr", axis=0, tiled=True),
        lax.all_gather(part_left, "nbr", axis=0, tiled=True),
        lax.all_gather(part_right, "nbr", axis=0, tiled=True),
        lax.all_gather(part_own, "nbr", axis=0, tiled=True),
    )
    masked = near_band * pair_mask.astype(jnp.float32)[:, :, None, None, None]
    local_slots = near_band.shape[1]
    windows = []
    widened = extended_2(masked, (("box", 0),), REACH)
    for slot_index in range(local_slots):
        windows.append((widened[:, slot_index], REACH))
    extended = jnp.zeros((box_count + 2 * REACH, SKEL, SKEL), jnp.float32)
    couples = []
    for slot_index in range(local_slots):
        window, margin = windows[slot_index]
        global_slot = nbr_place * local_slots + slot_index
        offset = jnp.where(global_slot < REACH, global_slot - REACH, global_slot - REACH + 1)
        near_piece = lax.dynamic_slice_in_dim(window, margin - offset, box_count, 0)
        coupled, update = slot_terms(near_piece, chooser, interp, approx, left_factor, right_factor)
        couples.append(coupled)
        extended = extended + lax.dynamic_update_slice_in_dim(
            jnp.zeros_like(extended), update, REACH - offset, 0
        )
    incoming_right = passed_along(extended[:REACH], "box", -1)
    incoming_left = passed_along(extended[REACH + box_count :], "box", 1)
    owned_sum = extended[REACH : REACH + box_count]
    owned_sum = owned_sum.at[box_count - REACH :].add(incoming_right)
    owned_sum = owned_sum.at[:REACH].add(incoming_left)
    update_total = lax.psum(owned_sum, "nbr")
    skeleton_self = own_block - update_total
    row_count = approx.shape[1] // nbr_count
    red_inverse = lax.dynamic_slice_in_dim(approx, nbr_place * row_count, row_count, 1)
    return (skeleton_self, red_inverse, jnp.stack(couples, 1))


def solution(mesh):
    placed = (
        P("box", "nbr", None),
        P("box", None),
        P("box", None, None),
        P("box", "nbr", None, None, None),
        P("box", "nbr"),
    )
    return jax.shard_map(
        body,
        mesh=mesh,
        in_specs=placed,
        out_specs=(P("box", None, None), P("box", "nbr", None), P("box", "nbr", None, None)),
        check_vma=False,
    )
```

profile of v0, /device:TPU:0, one launch (start us, length us, event | category | flops | bytes accessed | tf_op | source)
XLA Modules:
  0.0 154.4 jit_solution(4811347467437603980)
XLA Ops:
  7.2 4.4 %all-to-all-start = ((f32[8,64,256]{2,1,0:T(8,128)}), f32[8,64,256]{2,1,0:T(8,128)S(1)}, u32[]{:S(2)}, u32[]{:S(2)}) async-start(f32[8,64,256]{2,1,0:T(8,128)} %param.9), calls=%async_computation | async-start | bytes 1048576 | tf_op jit(solution)/shard_map/all_to_all | solution.py:97
  12.3 1.9 %broadcast_multiply_fusion = f32[8,2,2,64,256]{4,3,2,1,0:T(8,128)S(1)} fusion(f32[8,2,2,64,256]{4,3,2,1,0:T(8,128)} %param.12, f32[8,2]{1,0:T(8,128)S(1)} %copy.79), kind=kLoop, calls=%fused_computation.31 | loop fusion | flops 524288 | bytes 4194368 | tf_op jit(solution)/shard_map/mul | solution.py:107
  14.2 1.5 fusion.50
  15.8 2.3 %collective-permute-start = (f32[4,2,2,64,256]{4,3,2,1,0:T(8,128)}, f32[4,2,2,64,256]{4,3,2,1,0:T(8,128)}, u32[]{:S(2)}, u32[]{:S(2)}) collective-permute-start(f32[4,2,2,64,256]{4,3,2,1,0:T(8,128)} %get-tuple-element.44), channel_id=1, source_target_pairs={{0,4},{4,8},{8,12},{12,16},{16,20},{20,24},{24,28},{28,0},{1,5},{5... | collective-permute-start | bytes 3145736 | tf_op jit(solution)/shard_map/ppermute | solution.py:18
  18.1 3.0 %collective-permute-start.1 = (f32[4,2,2,64,256]{4,3,2,1,0:T(8,128)}, f32[4,2,2,64,256]{4,3,2,1,0:T(8,128)}, u32[]{:S(2)}, u32[]{:S(2)}) collective-permute-start(f32[4,2,2,64,256]{4,3,2,1,0:T(8,128)} %get-tuple-element.45), channel_id=1, source_target_pairs={{4,0},{8,4},{12,8},{16,12},{20,16},{24,20},{28,24},{0,28},{5,1},{9... | collective-permute-start | bytes 3145736 | tf_op jit(solution)/shard_map/ppermute | solution.py:21
  21.8 1.1 iota_compare_fusion
  23.0 1.4 fusion.12
  24.3 1.3 fusion.10
  29.3 10.5 %copy.75 = f32[2,192,192]{0,2,1:T(8,128)} copy(f32[2,192,192]{2,1,0:T(8,128)} %slice.151) | data formatting | bytes 589824 | tf_op jit(solution)/shard_map/slice | solution.py:51
  39.8 5.2 %gather_fusion = f32[192,2]{1,0:T(8,128)} fusion(f32[2,192,192]{0,2,1:T(8,128)} %copy.75, s32[192]{0:T(256)S(1)} %bitcast.80), kind=kCustom, calls=%fused_computation | custom fusion | bytes 4608 | tf_op jit(solution)/shard_map/jit(diagonal)/gather | solution.py:62
  45.0 1.0 copy.76
  46.0 1.5 convolution_add_fusion
  47.5 1.5 fusion.14
  51.7 2.1 %fusion.28 = f32[2,64,192]{2,1,0:T(8,128)} fusion(f32[2,192,192]{2,1,0:T(8,128)S(1)} %convolution_subtract_fusion.6, f32[2,64,192]{2,1,0:T(8,128)} %fusion.36, f32[2,256,256]{2,1,0:T(8,128)S(1)} %fusion.10), kind=kOutput, calls=%fused_computation.61 | convolution fusion | flops 56647680 | bytes 720896 | tf_op jit(solution)/shard_map/bij,bjk->bik/dot_general | solution.py:33
  53.9 1.8 %copy.96 = f32[2,192,64]{1,2,0:T(8,128)} copy(f32[2,192,64]{2,1,0:T(8,128)} %slice.152) | data formatting | bytes 196608
  55.6 1.2 convolution_subtract_fusion.13
  56.9 1.2 convolution_subtract_fusion.14
  58.0 7.4 %all_gather.12 = f32[8,64,64]{2,1,0:T(8,128)} all-gather(f32[2,64,64]{2,1,0:T(8,128)S(1)} %convolution_subtract_fusion.14), channel_id=1, replica_groups=mesh['box'=8,'nbr'=4] {'nbr'}, dimensions={0}, use_global_device_ids=true | all-gather | bytes 163840 | tf_op jit(solution)/shard_map/all_gather | solution.py:105
  65.4 10.1 %all_gather.14 = f32[8,64,192]{2,1,0:T(8,128)S(1)} all-gather(f32[2,64,192]{2,1,0:T(8,128)} %fusion.28), channel_id=1, replica_groups=mesh['box'=8,'nbr'=4] {'nbr'}, dimensions={0}, use_global_device_ids=true | all-gather | bytes 491520 | tf_op jit(solution)/shard_map/all_gather | solution.py:103
  76.0 7.5 %all_gather.15 = f32[8,192,64]{1,2,0:T(8,128)S(1)} all-gather(f32[2,192,64]{1,2,0:T(8,128)S(1)} %fusion.56), channel_id=1, replica_groups=mesh['box'=8,'nbr'=4] {'nbr'}, dimensions={0}, use_global_device_ids=true | all-gather | bytes 491520 | tf_op jit(solution)/shard_map/all_gather | solution.py:104
  83.5 2.0 %pad_maximum_fusion = f32[16,2,2,64,256]{4,3,2,1,0:T(8,128)S(1)} fusion(f32[4,2,2,64,256]{4,3,2,1,0:T(8,128)} %collective-permute-done.1, f32[8,2,2,64,256]{4,3,2,1,0:T(8,128)S(1)} %broadcast_multiply_fusion, f32[4,2,2,64,256]{4,3,2,1,0:T(8,128)} %collective-permute-done), kind=kLoop, calls=%fused_computation.1 | loop fusion | flops 2097152 | bytes 8388608 | tf_op jit(solution)/shard_map/concatenate | solution.py:22
  85.9 1.6 %fusion.2 = f32[8,2,64,256]{3,2,0,1:T(8,128)S(1)} fusion(s32[8,256]{1,0:T(8,128)S(1)} %copy-done.14, f32[16,1,2,64,256]{4,3,2,1,0:T(8,128)S(1)} %get-tuple-element.42, s32[]{:T(128)S(6)} %select_n.30), kind=kOutput, calls=%fused_computation.5 | convolution fusion | flops 805830656 | bytes 2105348 | tf_op jit(solution)/shard_map/bpik,bjk->bpij/dot_general | solution.py:33
  88.2 1.6 %fusion = f32[8,2,64,256]{3,2,1,0:T(8,128)S(1)} fusion(f32[16,1,2,64,256]{4,3,2,1,0:T(8,128)S(1)} %get-tuple-element.43, s32[]{:T(128)S(6)} %select_n.28, s32[8,256]{1,0:T(8,128)S(1)} %copy-done.14), kind=kOutput, calls=%fused_computation.3 | convolution fusion | flops 805830656 | bytes 2105348 | tf_op jit(solution)/shard_map/bpik,bjk->bpij/dot_general | solution.py:33
  94.4 1.1 maximum_bitcast_fusion
  95.5 2.8 %fusion.54 = f32[8,64,192]{2,1,0:T(8,128)S(1)} fusion(f32[8,64,192]{2,1,0:T(8,128)} %copy-done.4, f32[8,192,192]{2,1,0:T(8,128)} %all-gather.2.cloned.1.call-done), kind=kOutput, calls=%fused_computation.89 | convolution fusion | flops 226492416 | bytes 1966080 | tf_op jit(solution)/shard_map/bij,bjk->bik/dot_general | solution.py:33
  99.0 1.1 fusion.55
  101.7 2.3 %collective-permute-start.2 = (f32[4,64,64]{2,1,0:T(8,128)S(1)}, f32[4,64,64]{2,1,0:T(8,128)S(1)}, u32[]{:S(2)}, u32[]{:S(2)}) collective-permute-start(f32[4,64,64]{2,1,0:T(8,128)S(1)} %get-tuple-element.51), channel_id=1, source_target_pairs={{4,0},{8,4},{12,8},{16,12},{20,16},{24,20},{28,24},{0,28},{5,1},{9... | collective-permute-start | bytes 196616 | tf_op jit(solution)/shard_map/ppermute | solution.py:29
  103.9 1.1 pad_maximum_fusion.1
  105.0 2.4 %copy.87 = f32[8,2,64,128]{3,2,1,0:T(8,128)} copy(f32[8,2,64,128]{2,3,0,1:T(8,128)} %pad_maximum_fusion.1) | data formatting | bytes 1048576
  107.5 8.1 %collective-permute-done.3 = f32[4,64,64]{2,1,0:T(8,128)S(1)} collective-permute-done((f32[4,64,64]{2,1,0:T(8,128)S(1)}, f32[4,64,64]{2,1,0:T(8,128)S(1)}, u32[]{:S(2)}, u32[]{:S(2)}) %collective-permute-start.3) | collective-permute-done | bytes 65568 | tf_op jit(solution)/shard_map/ppermute | solution.py:29
  117.2 28.7 %all-reduce.2.cloned.1.call-done = f32[8,64,64]{2,1,0:T(8,128)} async-done(((f32[8,64,64]{2,1,0:T(8,128)}), f32[8,64,64]{2,1,0:T(8,128)}) %all-reduce.2.cloned.1.call-update) | async-done | bytes 131088 | tf_op jit(solution)/shard_map/psum | solution.py:130
  145.9 1.7 %sub.80 = f32[8,64,64]{2,1,0:T(8,128)} subtract(f32[8,64,64]{2,1,0:T(8,128)S(1)} %copy-done.12, f32[8,64,64]{2,1,0:T(8,128)} %all-reduce.2.cloned.1.call-done) | non-fusion elementwise | flops 32768 | bytes 393216 | tf_op jit(solution)/shard_map/sub | solution.py:131
  (75 shorter events, 17.7 us)
Async XLA Ops:
  7.2 18.5 %copy-start = (f32[8,64,192]{2,1,0:T(8,128)S(1)}, f32[8,64,192]{2,1,0:T(8,128)}, u32[]{:S(2)}) copy-start(f32[8,64,192]{2,1,0:T(8,128)} %param.11) | copy-start | bytes 1179652
  7.2 15.8 %all-to-all-start = ((f32[8,64,256]{2,1,0:T(8,128)}), f32[8,64,256]{2,1,0:T(8,128)S(1)}, u32[]{:S(2)}, u32[]{:S(2)}) async-start(f32[8,64,256]{2,1,0:T(8,128)} %param.9), calls=%async_computation | async-start | bytes 1048576 | tf_op jit(solution)/shard_map/all_to_all | solution.py:97
  11.6 83.9 %all-gather.2.cloned.1.call-start = ((), (), s32[]{:S(2)}) async-start(), calls=%async_computation.1 | async-start | bytes 1966080 | tf_op jit(solution)/shard_map/all_gather | solution.py:102
  14.2 7.6 %copy-start.14 = (s32[8,256]{1,0:T(8,128)S(1)}, s32[8,256]{1,0:T(8,128)}, u32[]{:S(2)}) copy-start(s32[8,256]{1,0:T(8,128)} %param.10) | copy-start | bytes 24580
  15.8 67.7 %collective-permute-start = (f32[4,2,2,64,256]{4,3,2,1,0:T(8,128)}, f32[4,2,2,64,256]{4,3,2,1,0:T(8,128)}, u32[]{:S(2)}, u32[]{:S(2)}) collective-permute-start(f32[4,2,2,64,256]{4,3,2,1,0:T(8,128)} %get-tuple-element.44), channel_id=1, source_target_pairs={{0,4},{4,8},{8,12},{12,16},{16,20},{20,24},{24,28},{28,0},{1,5},{5... | collective-permute-start | bytes 3145736 | tf_op jit(solution)/shard_map/ppermute | solution.py:18
  18.1 65.4 %collective-permute-start.1 = (f32[4,2,2,64,256]{4,3,2,1,0:T(8,128)}, f32[4,2,2,64,256]{4,3,2,1,0:T(8,128)}, u32[]{:S(2)}, u32[]{:S(2)}) collective-permute-start(f32[4,2,2,64,256]{4,3,2,1,0:T(8,128)} %get-tuple-element.45), channel_id=1, source_target_pairs={{4,0},{8,4},{12,8},{16,12},{20,16},{24,20},{28,24},{0,28},{5,1},{9... | collective-permute-start | bytes 3145736 | tf_op jit(solution)/shard_map/ppermute | solution.py:21
  46.0 3.0 %copy-start.13 = (f32[192,192]{1,0:T(8,128)S(1)}, f32[192,192]{1,0:T(8,128)}, u32[]{:S(2)}) copy-start(f32[192,192]{1,0:T(8,128)} %fusion.25) | copy-start | bytes 442372
  51.7 2.1 %copy-start.2 = (f32[2,192,192]{2,1,0:T(8,128)}, f32[2,192,192]{2,1,0:T(8,128)S(1)}, u32[]{:S(2)}) copy-start(f32[2,192,192]{2,1,0:T(8,128)S(1)} %convolution_subtract_fusion.6) | copy-start | bytes 884740
  53.8 21.7 %copy-start.3 = (f32[2,192,192]{2,1,0:T(8,128)S(1)}, f32[2,192,192]{2,1,0:T(8,128)}, u32[]{:S(2)}) copy-start(f32[2,192,192]{2,1,0:T(8,128)} %copy-done.2) | copy-start | bytes 884740
  53.8 92.0 %all-reduce.2.cloned.1.call-start = ((), (), s32[]{:S(2)}) async-start(), calls=%async_computation.2 | async-start | bytes 524288 | tf_op jit(solution)/shard_map/psum | solution.py:130
  88.2 3.5 %copy-start.5 = (f32[8,64,192]{2,1,0:T(8,128)}, f32[8,64,192]{2,1,0:T(8,128)S(1)}, u32[]{:S(2)}) copy-start(f32[8,64,192]{2,1,0:T(8,128)S(1)} %convolution_subtract_fusion) | copy-start | bytes 1179652
  91.7 2.0 %copy-start.4 = (f32[8,64,192]{2,1,0:T(8,128)}, f32[8,64,192]{2,1,0:T(8,128)S(1)}, u32[]{:S(2)}) copy-start(f32[8,64,192]{2,1,0:T(8,128)S(1)} %convolution_subtract_fusion.3) | copy-start | bytes 1179652
  95.5 3.5 %copy-start.1 = (f32[8,192,192]{2,1,0:T(8,128)S(1)}, f32[8,192,192]{2,1,0:T(8,128)}, u32[]{:S(2)}) copy-start(f32[8,192,192]{2,1,0:T(8,128)} %all-gather.2.cloned.1.call-done) | copy-start | bytes 3538948
  98.3 1.8 %copy-start.6 = (f32[8,64,192]{2,1,0:T(8,128)S(1)}, f32[8,64,192]{2,1,0:T(8,128)}, u32[]{:S(2)}) copy-start(f32[8,64,192]{2,1,0:T(8,128)} %copy-done.5) | copy-start | bytes 1179652
  99.0 4.9 %copy-start.9 = (f32[8,1,64,128]{2,3,0,1:T(8,128)S(1)}, f32[8,1,64,128]{2,3,0,1:T(8,128)}, u32[]{:S(2)}) copy-start(f32[8,1,64,128]{2,3,0,1:T(8,128)} %get-tuple-element.52) | copy-start | bytes 786436
  99.0 4.9 %copy-start.10 = (f32[8,1,64,128]{2,3,0,1:T(8,128)S(1)}, f32[8,1,64,128]{2,3,0,1:T(8,128)}, u32[]{:S(2)}) copy-start(f32[8,1,64,128]{2,3,0,1:T(8,128)} %get-tuple-element.53) | copy-start | bytes 786436
  100.8 0.8 copy-start.7
  101.7 5.7 %copy-start.8 = (f32[16,64,64]{2,1,0:T(8,128)S(1)}, f32[16,64,64]{2,1,0:T(8,128)}, u32[]{:S(2)}) copy-start(f32[16,64,64]{2,1,0:T(8,128)} %copy-done.7) | copy-start | bytes 786436
  101.7 5.8 %collective-permute-start.2 = (f32[4,64,64]{2,1,0:T(8,128)S(1)}, f32[4,64,64]{2,1,0:T(8,128)S(1)}, u32[]{:S(2)}, u32[]{:S(2)}) collective-permute-start(f32[4,64,64]{2,1,0:T(8,128)S(1)} %get-tuple-element.51), channel_id=1, source_target_pairs={{4,0},{8,4},{12,8},{16,12},{20,16},{24,20},{28,24},{0,28},{5,1},{9... | collective-permute-start | bytes 196616 | tf_op jit(solution)/shard_map/ppermute | solution.py:29
  105.0 40.9 %copy-start.12 = (f32[8,64,64]{2,1,0:T(8,128)S(1)}, f32[8,64,64]{2,1,0:T(8,128)}, u32[]{:S(2)}) copy-start(f32[8,64,64]{2,1,0:T(8,128)} %all_gather.12) | copy-start | bytes 393220
  107.4 8.2 %collective-permute-start.3 = (f32[4,64,64]{2,1,0:T(8,128)S(1)}, f32[4,64,64]{2,1,0:T(8,128)S(1)}, u32[]{:S(2)}, u32[]{:S(2)}) collective-permute-start(f32[4,64,64]{2,1,0:T(8,128)S(1)} %get-tuple-element.50), channel_id=1, source_target_pairs={{28,0},{0,4},{4,8},{8,12},{12,16},{16,20},{20,24},{24,28},{29,1},{... | collective-permute-start | bytes 196616 | tf_op jit(solution)/shard_map/ppermute | solution.py:29
  115.7 0.7 copy-start.11
Sparse Core Ops, SparseCore 0:
  53.9 20.9 all-gather.1
  116.5 29.3 all-reduce.1
where the time goes:
time: 155 us; the launch traced here: 154 us
  waiting for transfers between devices  36.9 us (24%)
  matrix products  28.6 us (18%)
  local copies, waits for them, and re-layouts  27.1 us (17%)
  blocking collectives  24.9 us (16%)
  between operations  14.5 us (9%)
  starting transfers between devices  12.1 us (8%)
  other arithmetic  10.3 us (7%)
    psum x1, waiting for transfers between devices, body(): update_total = lax.psum(owned_sum, 'nbr')  28.7 us
    dot_general x30, matrix products, product(): jnp.einsum(pattern, left_term, right_term, precision=lax.Precision.HIGHEST)  28.6 us
    slice x2, local copies, waits for them, and re-layouts, factors(): red_red = full_block[:, SKEL:, SKEL:]  11.4 us
    all_gather x1, blocking collectives, body(): lax.all_gather(part_left, 'nbr', axis=0, tiled=True)  10.1 us
    ppermute x2, waiting for transfers between devices, passed_along(): return lax.ppermute(block, axis, route)  8.12 us
    all_gather x1, blocking collectives, body(): lax.all_gather(part_right, 'nbr', axis=0, tiled=True)  7.46 us
    all_gather x1, blocking collectives, body(): lax.all_gather(part_own, 'nbr', axis=0, tiled=True)  7.4 us
    unnamed x33, local copies, waits for them, and re-layouts  6.4 us
  transfers between devices with their start and end apart: 7, of which 2 were waited for; matrix products, arithmetic and copies ran while one was open for 37% of the time, Pallas kernels for 0%

commit v1 on v0

v1 whole, which is shorter than its diff:
```python
import functools

import jax
import jax.numpy as jnp
from jax import lax
from jax.experimental import pallas as pl
from jax.experimental.pallas import tpu as pltpu
from jax.sharding import PartitionSpec as P

REACH = 4
NS_ITERS = 3
MESH = pl.DeviceIdType.MESH
NN = (((1,), (0,)), ((), ()))
NT = (((1,), (1,)), ((), ()))


def split(x):
    hi = x.astype(jnp.bfloat16)
    return hi, (x - hi.astype(jnp.float32)).astype(jnp.bfloat16)


def dot(a, b, dims=NN):
    return lax.dot_general(a, b, dims, preferred_element_type=jnp.float32)


def dot3(a, b, dims=NN):
    return dot(a[0], b[0], dims) + (dot(a[0], b[1], dims) + dot(a[1], b[0], dims))


def kernel(
    box_devs, nbr_devs, skel,
    self_ref, order_ref, interp_ref, band_ref, mask_ref,
    skel_out, inv_out, coup_out,
    blocks, bands, mask_far, y_buf, d_hi, d_lo, fac_hi, fac_lo, own, sums, arrived, others,
    a_own, a_send, a_recv, band_sem, band_send, mask_sem, u_sem, n_send, n_recv,
):
    boxes, rows, pts = self_ref.shape
    red = pts - skel
    slots = band_ref.shape[1]
    place = lax.axis_index("box")
    q = lax.axis_index("nbr")
    down = lax.rem(place + box_devs - 1, box_devs)
    up = lax.rem(place + 1, box_devs)
    first_half = q * slots < REACH
    pair, across, corner = (
        q + 1 - 2 * (q % 2),
        lax.rem(q + 2, 4),
        lax.rem(q + 2, 4) + 1 - 2 * (q % 2),
    )

    barrier = pltpu.get_barrier_semaphore()
    for other in (pair, across, corner):
        pl.semaphore_signal(barrier, inc=1, device_id=(place, other), device_id_type=MESH)
    for other in (down, up):
        pl.semaphore_signal(barrier, inc=1, device_id=(other, q), device_id_type=MESH)
    pl.semaphore_wait(barrier, 5)

    def my_rows(owner):
        return pl.ds(pl.multiple_of(owner * rows, rows), rows)

    def box_at(step):
        return jnp.where(first_half, boxes - 1 - step, step)

    def own_copy(b):
        return pltpu.make_async_copy(
            self_ref.at[b], blocks.at[b, my_rows(q)], a_own.at[b])

    def row_copy(b, kind, source_owner, target):
        src = self_ref.at[b] if kind < 2 else blocks.at[b, my_rows(source_owner)]
        return pltpu.make_async_remote_copy(
            src_ref=src, dst_ref=blocks.at[b, my_rows(source_owner)],
            send_sem=a_send.at[kind, b], recv_sem=a_recv.at[kind, b],
            device_id=(place, target), device_id_type=MESH)

    def row_wait(b, kind, source_owner):
        return pltpu.make_async_remote_copy(
            src_ref=blocks.at[b, my_rows(source_owner)],
            dst_ref=blocks.at[b, my_rows(source_owner)],
            send_sem=a_send.at[kind, b], recv_sem=a_recv.at[kind, b],
            device_id=(place, pair), device_id_type=MESH)

    far_device = jnp.where(first_half, down, up)
    near_device = jnp.where(first_half, up, down)

    def offset_of(s):
        slot = q * slots + s
        return jnp.where(slot < REACH, slot - REACH, slot - REACH + 1)

    mask_copy = pltpu.make_async_remote_copy(
        src_ref=mask_ref, dst_ref=mask_far, send_sem=mask_sem.at[0],
        recv_sem=mask_sem.at[1], device_id=(far_device, q), device_id_type=MESH)

    def band_far(b, s, source):
        return pltpu.make_async_remote_copy(
            src_ref=band_ref.at[source, s], dst_ref=bands.at[b, s],
            send_sem=band_send.at[b, s], recv_sem=band_sem.at[b, s],
            device_id=(far_device, q), device_id_type=MESH)

    def band_near(b, s, source):
        return pltpu.make_async_copy(
            band_ref.at[source, s], bands.at[b, s], band_sem.at[b, s])

    def is_far(b, s):
        c = b - offset_of(s)
        return (c < 0) | (c >= boxes)

    def source_of(b, s):
        return lax.rem(b - offset_of(s) + boxes, boxes)

    def start(step, carry):
        for_across = jnp.where(first_half, step, boxes - 1 - step)
        row_copy(for_across, 1, q, across).start()
        b = box_at(step)
        row_copy(b, 0, q, pair).start()
        own_copy(b).start()
        return carry

    mask_copy.start()
    lax.fori_loop(0, boxes, start, 0)

    def start_band(step, carry):
        b = box_at(step)
        for s in range(slots):
            @pl.when(is_far(b, s))
            def _():
                band_far(b, s, source_of(b, s)).start()

            @pl.when(jnp.logical_not(is_far(b, s)))
            def _():
                band_near(b, s, source_of(b, s)).start()
        return carry

    lax.fori_loop(0, boxes, start_band, 0)
    sums[...] = jnp.zeros_like(sums)

    lane = lax.broadcasted_iota(jnp.int32, (pts, pts), 1)
    sub = lax.broadcasted_iota(jnp.int32, (pts, pts), 0)
    on_diag = sub == lane
    red_diag = lax.broadcasted_iota(jnp.int32, (red, red), 0) == lax.broadcasted_iota(
        jnp.int32, (red, red), 1)

    def forward(b):
        row_wait(b, 1, across).wait_recv()
        row_copy(b, 2, across, pair).start()

    def factor(step, carry):
        b = box_at(step)

        @pl.when(step == 0)
        def _():
            forward(b)

        @pl.when(step + 1 < boxes)
        def _():
            forward(box_at(step + 1))

        order_row = order_ref[pl.ds(b, 1), :].astype(jnp.float32)
        order_col = jnp.broadcast_to(order_row, (8, pts)).T[:, 0:1].astype(jnp.int32)
        chosen = order_col == lane
        one_hot = jnp.where(chosen, 1.0, 0.0)
        t_hi, t_lo = split(interp_ref[b].T)
        skel_hot = one_hot[:skel].astype(jnp.bfloat16)
        spread_hi = dot(t_hi, skel_hot)
        spread_lo = dot(t_lo, skel_hot)
        d_hi[b] = jnp.concatenate([one_hot[:skel], one_hot[skel:] - spread_hi], 0).astype(jnp.bfloat16)
        d_lo[b] = -spread_lo.astype(jnp.bfloat16)
        dh, dl = d_hi[b], d_lo[b]

        own_copy(b).wait()
        row_wait(b, 0, pair).wait_recv()
        row_wait(b, 2, corner).wait_recv()
        matrix = blocks[b]
        diag_row = jnp.sum(jnp.where(on_diag, matrix, 0.0), axis=0, keepdims=True)
        diag_col = jnp.sum(jnp.where(chosen[skel:], diag_row, 0.0), axis=1, keepdims=True)
        inv_col = 1.0 / diag_col
        start_y = jnp.where(red_diag, inv_col, 0.0)
        inv_row = jnp.sum(start_y, axis=0, keepdims=True)

        m_hi, m_lo = split(matrix)
        left = dot(dh, m_hi) + dot(dh, m_lo)
        left = jnp.concatenate([left[:skel], left[skel:] + dot(dl, m_hi)], 0)
        v_hi, v_lo = split(left)
        right = dot(v_hi, dh, NT) + dot(v_lo, dh, NT)
        fix = dot(v_hi, dl, NT)
        skel_skel = right[:skel, :skel]
        x_sr = right[:skel, skel:] + fix[:skel]
        x_rs = right[skel:, :skel]
        x_rr = right[skel:, skel:] + fix[skel:]
        xrr = split(x_rr)
        y = 2.0 * start_y - inv_col * (x_rr * inv_row)
        for _ in range(NS_ITERS - 1):
            ys = split(y)
            y = 2.0 * y - dot3(ys, split(dot3(xrr, ys)))
        ys = split(y)
        xrs = split(x_rs)
        left_factor = dot3(split(x_sr), ys)
        right_factor = dot3(ys, xrs)
        lf = split(left_factor)
        own_block = skel_skel - dot3(lf, xrs)
        rt = split(right_factor.T)
        fac_hi[b] = jnp.concatenate([lf[0], rt[0], ys[0]], 0)
        fac_lo[b] = jnp.concatenate([lf[1], rt[1], ys[1]], 0)
        own[b] = own_block
        y_buf[...] = y
        part = red // nbr_devs
        inv_out[b] = y_buf[pl.ds(pl.multiple_of(q * part, 8), part)]
        return carry

    def done_sends(step, carry):
        b = box_at(step)
        row_copy(b, 2, across, pair).wait_send()
        row_copy(b, 1, q, across).wait_send()
        row_copy(b, 0, q, pair).wait_send()
        return carry

    lax.fori_loop(0, boxes, factor, 0)
    lax.fori_loop(0, boxes, done_sends, 0)
    mask_copy.wait()

    half = lax.rem(lax.broadcasted_iota(jnp.int32, (skel, slots * 2 * skel), 1), 2 * skel) < skel

    def slot_step(step, carry):
        b = box_at(step)
        pieces = []
        for s in range(slots):
            band_near(b, s, 0).wait()
            c = source_of(b, s)
            far = is_far(b, s).astype(jnp.int32)
            weight = far * mask_far[pl.ds(c, 1), s : s + 1] + (1 - far) * mask_ref[pl.ds(c, 1), s : s + 1]
            weight = weight.astype(jnp.float32)
            pieces += [bands[b, s, 1] * weight, bands[b, s, 0] * weight]
        b_hi, b_lo = split(jnp.concatenate(pieces, 0))
        dh, dl = d_hi[b], d_lo[b]
        turned = dot(dh, b_hi, NT) + dot(dh, b_lo, NT)
        skel_part = turned[:skel]
        red_part = turned[skel:] + dot(dl, b_hi, NT)
        f = dot3((fac_hi[b], fac_lo[b]), split(red_part))
        coupled = skel_part - jnp.where(half, f[:skel], f[skel : 2 * skel])
        flipped = red_part.T
        z = split(f[2 * skel :])
        near_red = split(jnp.concatenate(
            [flipped[(2 * s + 1) * skel : (2 * s + 2) * skel] for s in range(slots)], 0))
        u = dot3(near_red, z)
        for s in range(slots):
            coup_out[b, s] = coupled[:, 2 * s * skel : 2 * (s + 1) * skel]
            one = u[s * skel : (s + 1) * skel, 2 * s * skel : (2 * s + 1) * skel]
            packed = jnp.concatenate([one[: skel // 2], one[skel // 2 :]], 1)
            at = b - offset_of(s) + REACH
            sums[at] = sums[at] + packed
        return carry

    lax.fori_loop(0, REACH, slot_step, 0)
    leaving = jnp.where(first_half, boxes + REACH, 0)
    u_copy = pltpu.make_async_remote_copy(
        src_ref=sums.at[pl.ds(leaving, REACH)], dst_ref=arrived, send_sem=u_sem.at[0],
        recv_sem=u_sem.at[1], device_id=(near_device, q), device_id_type=MESH)
    u_copy.start()
    lax.fori_loop(REACH, boxes, slot_step, 0)
    u_copy.wait()
    landing = jnp.where(first_half, REACH, boxes)
    sums[pl.ds(landing, REACH)] = sums[pl.ds(landing, REACH)] + arrived[...]

    mine = sums.at[pl.ds(REACH, boxes)]
    copies = []
    for k, other in enumerate((pair, across, corner)):
        copies.append(pltpu.make_async_remote_copy(
            src_ref=mine, dst_ref=others.at[k], send_sem=n_send.at[k],
            recv_sem=n_recv.at[k], device_id=(place, other), device_id_type=MESH))
    for copy in copies:
        copy.start()

    def band_done(step, carry):
        b = box_at(step)
        for s in range(slots):
            @pl.when(is_far(b, s))
            def _():
                band_far(b, s, source_of(b, s)).wait_send()
        return carry

    lax.fori_loop(0, boxes, band_done, 0)
    for copy in copies:
        copy.wait()

    def finish(c, carry):
        total = (sums[c + REACH] + others[0, c]) + (others[1, c] + others[2, c])
        full = jnp.concatenate([total[:, :skel], total[:, skel:]], 0)
        skel_out[c] = own[c] - full
        return carry

    lax.fori_loop(0, boxes, finish, 0)


def body(box_devs, nbr_devs, self_block, ordering, interp, near_band, pair_mask):
    boxes, rows, pts = self_block.shape
    skel, red = interp.shape[1:]
    slots = near_band.shape[1]
    f32, bf16 = jnp.float32, jnp.bfloat16
    vmem = pl.BlockSpec(memory_space=pltpu.VMEM)
    hbm = pl.BlockSpec(memory_space=pl.ANY)
    dma = pltpu.SemaphoreType.DMA
    return pl.pallas_call(
        functools.partial(kernel, box_devs, nbr_devs, skel),
        out_shape=(
            jax.ShapeDtypeStruct((boxes, skel, skel), f32),
            jax.ShapeDtypeStruct((boxes, red // nbr_devs, red), f32),
            jax.ShapeDtypeStruct((boxes, slots, skel, 2 * skel), f32),
        ),
        in_specs=[hbm, vmem, vmem, hbm, vmem],
        out_specs=(vmem, vmem, vmem),
        scratch_shapes=[
            pltpu.VMEM((boxes, pts, pts), f32),
            pltpu.VMEM((boxes, slots, 2, skel, pts), f32),
            pltpu.VMEM(pair_mask.shape, jnp.int32),
            pltpu.VMEM((red, red), f32),
            pltpu.VMEM((boxes, pts, pts), bf16),
            pltpu.VMEM((boxes, red, pts), bf16),
            pltpu.VMEM((boxes, 2 * skel + red, red), bf16),
            pltpu.VMEM((boxes, 2 * skel + red, red), bf16),
            pltpu.VMEM((boxes, skel, skel), f32),
            pltpu.VMEM((boxes + 2 * REACH, skel // 2, 2 * skel), f32),
            pltpu.VMEM((REACH, skel // 2, 2 * skel), f32),
            pltpu.VMEM((nbr_devs - 1, boxes, skel // 2, 2 * skel), f32),
            dma((boxes,)),
            dma((3, boxes)),
            dma((3, boxes)),
            dma((boxes, slots)),
            dma((boxes, slots)),
            dma((2,)),
            dma((2,)),
            dma((nbr_devs - 1,)),
            dma((nbr_devs - 1,)),
        ],
        compiler_params=pltpu.CompilerParams(
            collective_id=0, has_side_effects=True, vmem_limit_bytes=56 * 1024 * 1024),
        name="level",
    )(self_block, ordering, interp, near_band, pair_mask)


def solution(mesh):
    placed = (
        P("box", "nbr", None),
        P("box", None),
        P("box", None, None),
        P("box", "nbr", None, None, None),
        P("box", "nbr"),
    )
    return jax.shard_map(
        functools.partial(body, mesh.shape["box"], mesh.shape["nbr"]),
        mesh=mesh,
        in_specs=placed,
        out_specs=(P("box", None, None), P("box", "nbr", None), P("box", "nbr", None, None)),
        check_vma=False,
    )
```

time: 155 us -> 58.7 us (0.38)
  Pallas kernels: 0 us -> 50.8 us
  waiting for transfers between devices: 36.9 us -> 0 us
  matrix products: 28.6 us -> 0 us
  blocking collectives: 24.9 us -> 0 us
  local copies, waits for them, and re-layouts: 27.1 us -> 6.67 us
  between operations: 14.5 us -> 0.64 us
  starting transfers between devices: 12.1 us -> 0 us
  other arithmetic: 10.3 us -> 0 us
    pallas_call x0 -> x1, Pallas kernels: none -> 50.8 us  [body(): pl.pallas_call(functools.partial(kernel, box_devs, nbr_devs, skel), out_s...]
    psum x1 -> x0, waiting for transfers between devices: 28.7 us -> none  [body(): update_total = lax.psum(owned_sum, 'nbr')]
    dot_general x30 -> x0, matrix products: 28.6 us -> none  [product(): jnp.einsum(pattern, left_term, right_term, precision=lax.Precision.HIGHEST)]
    all_gather x3 -> x0, blocking collectives: 24.9 us -> none  [the longest x1 10.1 us: body(): lax.all_gather(part_left, 'nbr', axis=0, tiled=True)]
    slice x6 -> x0, local copies, waits for them, and re-layouts: 13.4 us -> none  [the longest x2 11.4 us: factors(): red_red = full_block[:, SKEL:, SKEL:]]
    ppermute x4 -> x0, waiting for transfers between devices: 8.13 us -> none  [the longest x2 8.12 us: passed_along(): return lax.ppermute(block, axis, route)]
    ppermute x4 -> x0, starting transfers between devices: 7.64 us -> none  [the longest x1 3.04 us: extended_2(): lax.ppermute(lax.slice_in_dim(block, 0, width, axis=dim), axis, backward)]
    gather x2 -> x0, local copies, waits for them, and re-layouts: 6.2 us -> none  [factors(): diag_vals = jnp.diagonal(red_red, axis1=1, axis2=2)]
  transfers between devices with their start and end apart: 7 -> 0, of which waited for: 2 -> 0; matrix products, arithmetic and copies ran while one was open for 37% -> 0% of each run, Pallas kernels for 0% -> 0%
where the time goes in v1:
time: 58.7 us; the launch traced here: 58.1 us
  Pallas kernels  50.8 us (87%)
  local copies, waits for them, and re-layouts  6.67 us (11%)
  between operations  0.64 us (1%)
    pallas_call x1, Pallas kernels, body(): pl.pallas_call(functools.partial(kernel, box_devs, nbr_devs, skel), out_s...  50.8 us
    unnamed x4, local copies, waits for them, and re-layouts  6.67 us

profile of v1, /device:TPU:0, one launch (start us, length us, event | category | flops | bytes accessed | tf_op | source)
XLA Modules:
  0.0 58.1 jit_solution(7844409807911800085)
XLA Ops:
  0.6 1.3 %copy.8.mask_ref = s32[8,2]{1,0:T(8,128)} copy(s32[8,2]{0,1:T(2,128)} %param.9) | data formatting | bytes 128 | tf_op args[4]
  2.0 50.8 %level.1 = (f32[8,64,64]{2,1,0:T(8,128)}, f32[8,48,192]{2,1,0:T(8,128)}, f32[8,2,64,128]{3,2,1,0:T(8,128)}) custom-call(f32[8,64,256]{2,1,0:T(8,128)} %self_ref.1, s32[8,256]{1,0:T(8,128)} %order_ref.1, f32[8,64,192]{2,1,0:T(8,128)} %interp_ref.1, f32[8,2,2,64,256]{4,3,2,1,0:T(8,128)} %band_ref.1, s32[8,2]{1,0:T(8,128)} %copy.8.mask_ref), custom_call_target="tpu_custom_call" | custom-call | tf_op jit(solution)/shard_map/level/pallas_call | solution.py:301
  52.8 1.7 %copy.12 = f32[8,64,64]{2,1,0:T(8,128)} copy(f32[8,64,64]{2,1,0:T(8,128)} %get-tuple-element.6) | data formatting | bytes 262144
  54.5 1.8 %copy.13 = f32[8,48,192]{2,1,0:T(8,128)} copy(f32[8,48,192]{2,1,0:T(8,128)} %get-tuple-element.7) | data formatting | bytes 589824
  56.3 1.9 %copy.14 = f32[8,2,64,128]{3,2,1,0:T(8,128)} copy(f32[8,2,64,128]{3,2,1,0:T(8,128)} %get-tuple-element.8) | data formatting | bytes 1048576

commit v2 on v1

--- a/solution.py
+++ b/solution.py
@@ -53,13 +53,13 @@
         pl.semaphore_signal(barrier, inc=1, device_id=(place, other), device_id_type=MESH)
     for other in (down, up):
         pl.semaphore_signal(barrier, inc=1, device_id=(other, q), device_id_type=MESH)
-    pl.semaphore_wait(barrier, 5)
 
     def my_rows(owner):
         return pl.ds(pl.multiple_of(owner * rows, rows), rows)
 
     def box_at(step):
-        return jnp.where(first_half, boxes - 1 - step, step)
+        spot = jnp.where(step == 0, REACH, jnp.where(step <= REACH, step - 1, step))
+        return jnp.where(first_half, boxes - 1 - spot, spot)
 
     def own_copy(b):
         return pltpu.make_async_copy(
@@ -108,29 +108,29 @@
         return lax.rem(b - offset_of(s) + boxes, boxes)
 
     def start(step, carry):
-        for_across = jnp.where(first_half, step, boxes - 1 - step)
-        row_copy(for_across, 1, q, across).start()
-        b = box_at(step)
+        b = box_at(step)
+        row_copy(boxes - 1 - b, 1, q, across).start()
         row_copy(b, 0, q, pair).start()
+        return carry
+
+    def start_near(step, carry):
+        b = box_at(step)
         own_copy(b).start()
-        return carry
-
-    mask_copy.start()
-    lax.fori_loop(0, boxes, start, 0)
-
-    def start_band(step, carry):
+        for s in range(slots):
+            @pl.when(jnp.logical_not(is_far(b, s)))
+            def _():
+                band_near(b, s, source_of(b, s)).start()
+        return carry
+
+    def start_far(step, carry):
         b = box_at(step)
         for s in range(slots):
             @pl.when(is_far(b, s))
             def _():
                 band_far(b, s, source_of(b, s)).start()
-
-            @pl.when(jnp.logical_not(is_far(b, s)))
-            def _():
-                band_near(b, s, source_of(b, s)).start()
-        return carry
-
-    lax.fori_loop(0, boxes, start_band, 0)
+        return carry
+
+    lax.fori_loop(0, boxes, start_near, 0)
     sums[...] = jnp.zeros_like(sums)
 
     lane = lax.broadcasted_iota(jnp.int32, (pts, pts), 1)
@@ -143,29 +143,25 @@
         row_wait(b, 1, across).wait_recv()
         row_copy(b, 2, across, pair).start()
 
-    def factor(step, carry):
-        b = box_at(step)
-
-        @pl.when(step == 0)
-        def _():
-            forward(b)
-
-        @pl.when(step + 1 < boxes)
-        def _():
-            forward(box_at(step + 1))
-
+    def chosen_of(b):
         order_row = order_ref[pl.ds(b, 1), :].astype(jnp.float32)
-        order_col = jnp.broadcast_to(order_row, (8, pts)).T[:, 0:1].astype(jnp.int32)
-        chosen = order_col == lane
-        one_hot = jnp.where(chosen, 1.0, 0.0)
+        return jnp.broadcast_to(order_row, (8, pts)).T[:, 0:1].astype(jnp.int32) == lane
+
+    def prepare(step, carry):
+        b = box_at(step)
+        one_hot = jnp.where(chosen_of(b), 1.0, 0.0)
         t_hi, t_lo = split(interp_ref[b].T)
         skel_hot = one_hot[:skel].astype(jnp.bfloat16)
         spread_hi = dot(t_hi, skel_hot)
         spread_lo = dot(t_lo, skel_hot)
         d_hi[b] = jnp.concatenate([one_hot[:skel], one_hot[skel:] - spread_hi], 0).astype(jnp.bfloat16)
         d_lo[b] = -spread_lo.astype(jnp.bfloat16)
+        return carry
+
+    def factor(step):
+        b = box_at(step)
         dh, dl = d_hi[b], d_lo[b]
-
+        chosen = chosen_of(b)
         own_copy(b).wait()
         row_wait(b, 0, pair).wait_recv()
         row_wait(b, 2, corner).wait_recv()
@@ -204,7 +200,6 @@
         y_buf[...] = y
         part = red // nbr_devs
         inv_out[b] = y_buf[pl.ds(pl.multiple_of(q * part, 8), part)]
-        return carry
 
     def done_sends(step, carry):
         b = box_at(step)
@@ -213,21 +208,20 @@
         row_copy(b, 0, q, pair).wait_send()
         return carry
 
-    lax.fori_loop(0, boxes, factor, 0)
-    lax.fori_loop(0, boxes, done_sends, 0)
-    mask_copy.wait()
-
     half = lax.rem(lax.broadcasted_iota(jnp.int32, (skel, slots * 2 * skel), 1), 2 * skel) < skel
 
-    def slot_step(step, carry):
+    mask_lane = lax.broadcasted_iota(jnp.int32, (1, boxes), 1)
+
+    def slot_step(step):
         b = box_at(step)
         pieces = []
         for s in range(slots):
             band_near(b, s, 0).wait()
             c = source_of(b, s)
             far = is_far(b, s).astype(jnp.int32)
-            weight = far * mask_far[pl.ds(c, 1), s : s + 1] + (1 - far) * mask_ref[pl.ds(c, 1), s : s + 1]
-            weight = weight.astype(jnp.float32)
+            weight = far * mask_far[s : s + 1, :] + (1 - far) * mask_ref[s : s + 1, :]
+            weight = jnp.sum(
+                jnp.where(mask_lane == c, weight.astype(jnp.float32), 0.0), axis=1, keepdims=True)
             pieces += [bands[b, s, 1] * weight, bands[b, s, 0] * weight]
         b_hi, b_lo = split(jnp.concatenate(pieces, 0))
         dh, dl = d_hi[b], d_lo[b]
@@ -247,27 +241,74 @@
             packed = jnp.concatenate([one[: skel // 2], one[skel // 2 :]], 1)
             at = b - offset_of(s) + REACH
             sums[at] = sums[at] + packed
-        return carry
-
-    lax.fori_loop(0, REACH, slot_step, 0)
+
     leaving = jnp.where(first_half, boxes + REACH, 0)
+    landing = jnp.where(first_half, REACH, boxes)
     u_copy = pltpu.make_async_remote_copy(
         src_ref=sums.at[pl.ds(leaving, REACH)], dst_ref=arrived, send_sem=u_sem.at[0],
         recv_sem=u_sem.at[1], device_id=(near_device, q), device_id_type=MESH)
-    u_copy.start()
-    lax.fori_loop(REACH, boxes, slot_step, 0)
-    u_copy.wait()
-    landing = jnp.where(first_half, REACH, boxes)
-    sums[pl.ds(landing, REACH)] = sums[pl.ds(landing, REACH)] + arrived[...]
-
-    mine = sums.at[pl.ds(REACH, boxes)]
-    copies = []
-    for k, other in enumerate((pair, across, corner)):
-        copies.append(pltpu.make_async_remote_copy(
-            src_ref=mine, dst_ref=others.at[k], send_sem=n_send.at[k],
-            recv_sem=n_recv.at[k], device_id=(place, other), device_id_type=MESH))
-    for copy in copies:
-        copy.start()
+    spans = [jnp.abs(offset_of(s)) for s in range(slots)]
+    longest = functools.reduce(jnp.maximum, spans)
+    shortest = functools.reduce(jnp.minimum, spans)
+    peers = (across, corner, pair)
+
+    def ready_at(c):
+        seen = jnp.where(first_half, c, boxes - 1 - c)
+        last = boxes - 1 - jnp.maximum(seen - longest, 0)
+        last = jnp.where(seen >= shortest, jnp.maximum(last, REACH), REACH)
+        return jnp.where(seen < REACH, jnp.maximum(last, boxes - 2), last)
+
+    def sum_copy(k, c):
+        return pltpu.make_async_remote_copy(
+            src_ref=sums.at[c + REACH], dst_ref=others.at[k, c], send_sem=n_send.at[k, c],
+            recv_sem=n_recv.at[k, c], device_id=(place, peers[k]), device_id_type=MESH)
+
+    def main(step, carry):
+        factor(step)
+
+        @pl.when(step == 0)
+        def _():
+            forward(box_at(1))
+            mask_copy.wait()
+
+        slot_step(step)
+
+        @pl.when(step + 2 < boxes)
+        def _():
+            forward(box_at(step + 2))
+
+        @pl.when(step == REACH)
+        def _():
+            u_copy.start()
+
+        @pl.when(step == boxes - 2)
+        def _():
+            u_copy.wait()
+            sums[pl.ds(landing, REACH)] = sums[pl.ds(landing, REACH)] + arrived[...]
+
+        def share(c, carry):
+            @pl.when(ready_at(c) == step)
+            def _():
+                for k in range(len(peers)):
+                    sum_copy(k, c).start()
+            return carry
+
+        @pl.when(step >= REACH)
+        def _():
+            lax.fori_loop(0, boxes, share, 0)
+
+        return carry
+
+    early = 3
+    lax.fori_loop(0, early, prepare, 0)
+    pl.semaphore_wait(barrier, 5)
+    lax.fori_loop(0, boxes, start, 0)
+    mask_copy.start()
+    lax.fori_loop(0, boxes, start_far, 0)
+    lax.fori_loop(early, boxes, prepare, 0)
+    forward(box_at(0))
+    lax.fori_loop(0, boxes, main, 0)
+    lax.fori_loop(0, boxes, done_sends, 0)
 
     def band_done(step, carry):
         b = box_at(step)
@@ -278,16 +319,39 @@
         return carry
 
     lax.fori_loop(0, boxes, band_done, 0)
-    for copy in copies:
-        copy.wait()
 
     def finish(c, carry):
+        for k in range(len(peers)):
+            sum_copy(k, c).wait()
         total = (sums[c + REACH] + others[0, c]) + (others[1, c] + others[2, c])
         full = jnp.concatenate([total[:, :skel], total[:, skel:]], 0)
         skel_out[c] = own[c] - full
         return carry
 
     lax.fori_loop(0, boxes, finish, 0)
+
+
+def deliver_kernel(count, *refs):
+    sems = refs[-1]
+    copies = [
+        pltpu.make_async_copy(refs[n], refs[count + n], sems.at[n]) for n in range(count)]
+    for copy in copies:
+        copy.start()
+    for copy in copies:
+        copy.wait()
+
+
+def deliver(arrays):
+    anywhere = pl.BlockSpec(memory_space=pl.ANY)
+    return pl.pallas_call(
+        functools.partial(deliver_kernel, len(arrays)),
+        out_shape=tuple(jax.ShapeDtypeStruct(a.shape, a.dtype) for a in arrays),
+        in_specs=[anywhere] * len(arrays),
+        out_specs=[anywhere] * len(arrays),
+        scratch_shapes=[pltpu.SemaphoreType.DMA((len(arrays),))],
+        compiler_params=pltpu.CompilerParams(vmem_limit_bytes=1024 * 1024),
+        name="deliver",
+    )(*arrays)
 
 
 def body(box_devs, nbr_devs, self_block, ordering, interp, near_band, pair_mask):
@@ -296,9 +360,9 @@
     slots = near_band.shape[1]
     f32, bf16 = jnp.float32, jnp.bfloat16
     vmem = pl.BlockSpec(memory_space=pltpu.VMEM)
-    hbm = pl.BlockSpec(memory_space=pl.ANY)
+    hbm = pl.BlockSpec(memory_space=pltpu.HBM)
     dma = pltpu.SemaphoreType.DMA
-    return pl.pallas_call(
+    results = pl.pallas_call(
         functools.partial(kernel, box_devs, nbr_devs, skel),
         out_shape=(
             jax.ShapeDtypeStruct((boxes, skel, skel), f32),
@@ -310,7 +374,7 @@
         scratch_shapes=[
             pltpu.VMEM((boxes, pts, pts), f32),
             pltpu.VMEM((boxes, slots, 2, skel, pts), f32),
-            pltpu.VMEM(pair_mask.shape, jnp.int32),
+            pltpu.VMEM(pair_mask.shape[::-1], jnp.int32),
             pltpu.VMEM((red, red), f32),
             pltpu.VMEM((boxes, pts, pts), bf16),
             pltpu.VMEM((boxes, red, pts), bf16),
@@ -327,13 +391,14 @@
             dma((boxes, slots)),
             dma((2,)),
             dma((2,)),
-            dma((nbr_devs - 1,)),
-            dma((nbr_devs - 1,)),
+            dma((nbr_devs - 1, boxes)),
+            dma((nbr_devs - 1, boxes)),
         ],
         compiler_params=pltpu.CompilerParams(
-            collective_id=0, has_side_effects=True, vmem_limit_bytes=56 * 1024 * 1024),
+            collective_id=0, has_side_effects=True, vmem_limit_bytes=52 * 1024 * 1024),
         name="level",
-    )(self_block, ordering, interp, near_band, pair_mask)
+    )(self_block, ordering, interp, near_band, pair_mask.T)
+    return deliver(results)
 
 
 def solution(mesh):

time: 58.7 us -> 51 us (0.87)
  local copies, waits for them, and re-layouts: 6.67 us -> 2.41 us
  Pallas kernels: 50.8 us -> 47.6 us
    unnamed x4 -> x6, local copies, waits for them, and re-layouts: 6.67 us -> 2.41 us
    pallas_call x1, Pallas kernels: 50.8 us -> 46.6 us  [body(): pl.pallas_call(functools.partial(kernel, box_devs, nbr_devs, skel), out_s...]
    pallas_call x0 -> x1, Pallas kernels: none -> 1.04 us  [deliver(): pl.pallas_call(functools.partial(deliver_kernel, len(arrays)), out_shape=...]
where the time goes in v2:
time: 51 us; the launch traced here: 50.7 us
  Pallas kernels  47.6 us (93%)
  local copies, waits for them, and re-layouts  2.41 us (5%)
  between operations  0.65 us (1%)
    pallas_call x1, Pallas kernels, body(): pl.pallas_call(functools.partial(kernel, box_devs, nbr_devs, skel), out_s...  46.6 us
    unnamed x6, local copies, waits for them, and re-layouts  2.41 us
    pallas_call x1, Pallas kernels, deliver(): pl.pallas_call(functools.partial(deliver_kernel, len(arrays)), out_shape=...  1.04 us

profile of v2, /device:TPU:0, one launch (start us, length us, event | category | flops | bytes accessed | tf_op | source)
XLA Modules:
  0.0 50.7 jit_solution(12261985433477519363)
XLA Ops:
  0.6 0.0 copy-start
  0.6 1.0 %copy-done = f32[8,64,256]{2,1,0:T(8,128)S(1)} copy-done((f32[8,64,256]{2,1,0:T(8,128)S(1)}, f32[8,64,256]{2,1,0:T(8,128)}, u32[]{:S(2)}) %copy-start) | copy-done | bytes 524312
  1.7 0.0 copy-start.1
  1.7 0.7 %copy-done.1 = s32[8,256]{1,0:T(8,128)S(1)} copy-done((s32[8,256]{1,0:T(8,128)S(1)}, s32[8,256]{1,0:T(8,128)}, u32[]{:S(2)}) %copy-start.1) | copy-done | bytes 8216
  2.4 0.0 copy-start.2
  2.4 0.7 %copy-done.2 = s32[8,2]{0,1:T(2,128)S(1)} copy-done((s32[8,2]{0,1:T(2,128)S(1)}, s32[8,2]{0,1:T(2,128)}, u32[]{:S(2)}) %copy-start.2) | copy-done | bytes 88
  3.1 46.6 %level.1 = (f32[8,64,64]{2,1,0:T(8,128)S(1)}, f32[8,48,192]{2,1,0:T(8,128)S(1)}, f32[8,2,64,128]{3,2,1,0:T(8,128)S(1)}) custom-call(f32[8,64,256]{2,1,0:T(8,128)S(1)} %copy-done, s32[8,256]{1,0:T(8,128)S(1)} %copy-done.1, f32[8,64,192]{2,1,0:T(8,128)} %interp_ref.1, f32[8,2,2,64,256]{4,3,2,1,0:T(8,128)} %band_ref.1, s32[2,8]{1,0:T(2,128)S(1)} %bitcast.1), custom_call_target="tpu_custom_call" | custom-call | tf_op jit(solution)/shard_map/level/pallas_call | solution.py:365
  49.7 1.0 %deliver.1 = (f32[8,64,64]{2,1,0:T(8,128)}, f32[8,48,192]{2,1,0:T(8,128)}, f32[8,2,64,128]{3,2,1,0:T(8,128)}) custom-call(f32[8,64,64]{2,1,0:T(8,128)S(1)} %get-tuple-element.6.refs_0_, f32[8,48,192]{2,1,0:T(8,128)S(1)} %get-tuple-element.7.refs_1_, f32[8,2,64,128]{3,2,1,0:T(8,128)S(1)} %get-tuple-element.8.refs_2_), custom_call_target="tpu_custom_call" | custom-call | tf_op jit(solution)/shard_map/deliver/pallas_call | solution.py:346
Async XLA Ops:
  0.6 1.0 %copy-start = (f32[8,64,256]{2,1,0:T(8,128)S(1)}, f32[8,64,256]{2,1,0:T(8,128)}, u32[]{:S(2)}) copy-start(f32[8,64,256]{2,1,0:T(8,128)} %self_ref.1) | copy-start | bytes 1572868
  1.7 0.7 %copy-start.1 = (s32[8,256]{1,0:T(8,128)S(1)}, s32[8,256]{1,0:T(8,128)}, u32[]{:S(2)}) copy-start(s32[8,256]{1,0:T(8,128)} %order_ref.1) | copy-start | bytes 24580
  2.4 0.7 %copy-start.2 = (s32[8,2]{0,1:T(2,128)S(1)}, s32[8,2]{0,1:T(2,128)}, u32[]{:S(2)}) copy-start(s32[8,2]{0,1:T(2,128)} %param.9) | copy-start | bytes 196

commit v3 on v2

--- a/solution.py
+++ b/solution.py
@@ -58,8 +58,7 @@
         return pl.ds(pl.multiple_of(owner * rows, rows), rows)
 
     def box_at(step):
-        spot = jnp.where(step == 0, REACH, jnp.where(step <= REACH, step - 1, step))
-        return jnp.where(first_half, boxes - 1 - spot, spot)
+        return jnp.where(first_half, boxes - 1 - step, step)
 
     def own_copy(b):
         return pltpu.make_async_copy(
@@ -158,48 +157,53 @@
         d_lo[b] = -spread_lo.astype(jnp.bfloat16)
         return carry
 
-    def factor(step):
-        b = box_at(step)
-        dh, dl = d_hi[b], d_lo[b]
-        chosen = chosen_of(b)
-        own_copy(b).wait()
-        row_wait(b, 0, pair).wait_recv()
-        row_wait(b, 2, corner).wait_recv()
-        matrix = blocks[b]
-        diag_row = jnp.sum(jnp.where(on_diag, matrix, 0.0), axis=0, keepdims=True)
-        diag_col = jnp.sum(jnp.where(chosen[skel:], diag_row, 0.0), axis=1, keepdims=True)
-        inv_col = 1.0 / diag_col
-        start_y = jnp.where(red_diag, inv_col, 0.0)
-        inv_row = jnp.sum(start_y, axis=0, keepdims=True)
-
-        m_hi, m_lo = split(matrix)
-        left = dot(dh, m_hi) + dot(dh, m_lo)
-        left = jnp.concatenate([left[:skel], left[skel:] + dot(dl, m_hi)], 0)
-        v_hi, v_lo = split(left)
-        right = dot(v_hi, dh, NT) + dot(v_lo, dh, NT)
-        fix = dot(v_hi, dl, NT)
-        skel_skel = right[:skel, :skel]
-        x_sr = right[:skel, skel:] + fix[:skel]
-        x_rs = right[skel:, :skel]
-        x_rr = right[skel:, skel:] + fix[skel:]
-        xrr = split(x_rr)
-        y = 2.0 * start_y - inv_col * (x_rr * inv_row)
+    def each(f, *lists):
+        return [f(*items) for items in zip(*lists)]
+
+    def factor(bs):
+        dh = [d_hi[b] for b in bs]
+        dl = [d_lo[b] for b in bs]
+        for b in bs:
+            own_copy(b).wait()
+            row_wait(b, 0, pair).wait_recv()
+            row_wait(b, 2, corner).wait_recv()
+        matrix = [blocks[b] for b in bs]
+        ms = each(split, matrix)
+        left = each(lambda d, m: dot(d, m[0]) + dot(d, m[1]), dh, ms)
+        left = each(lambda l, d, m: jnp.concatenate(
+            [l[:skel], l[skel:] + dot(d, m[0])], 0), left, dl, ms)
+        vs = each(split, left)
+        right = each(lambda v, d: dot(v[0], d, NT) + dot(v[1], d, NT), vs, dh)
+        fix = each(lambda v, d: dot(v[0], d, NT), vs, dl)
+        x_rr = each(lambda r, f: r[skel:, skel:] + f[skel:], right, fix)
+        xrr = each(split, x_rr)
+        y = []
+        for n, b in enumerate(bs):
+            diag_row = jnp.sum(jnp.where(on_diag, matrix[n], 0.0), axis=0, keepdims=True)
+            diag_col = jnp.sum(
+                jnp.where(chosen_of(b)[skel:], diag_row, 0.0), axis=1, keepdims=True)
+            inv_col = 1.0 / diag_col
+            start_y = jnp.where(red_diag, inv_col, 0.0)
+            inv_row = jnp.sum(start_y, axis=0, keepdims=True)
+            y.append(2.0 * start_y - inv_col * (x_rr[n] * inv_row))
+        ys = each(split, y)
         for _ in range(NS_ITERS - 1):
-            ys = split(y)
-            y = 2.0 * y - dot3(ys, split(dot3(xrr, ys)))
-        ys = split(y)
-        xrs = split(x_rs)
-        left_factor = dot3(split(x_sr), ys)
-        right_factor = dot3(ys, xrs)
-        lf = split(left_factor)
-        own_block = skel_skel - dot3(lf, xrs)
-        rt = split(right_factor.T)
-        fac_hi[b] = jnp.concatenate([lf[0], rt[0], ys[0]], 0)
-        fac_lo[b] = jnp.concatenate([lf[1], rt[1], ys[1]], 0)
-        own[b] = own_block
-        y_buf[...] = y
+            xy = each(split, each(dot3, xrr, ys))
+            y = each(lambda a, p: 2.0 * a - p, y, each(dot3, ys, xy))
+            ys = each(split, y)
+        xrs = each(lambda r: split(r[skel:, :skel]), right)
+        xsr = each(lambda r, f: split(r[:skel, skel:] + f[:skel]), right, fix)
+        rt = each(lambda a, x: split(dot3(a, x).T), ys, xrs)
+        lf = each(split, each(dot3, xsr, ys))
+        owned = each(lambda r, l, x: r[:skel, :skel] - dot3(l, x), right, lf, xrs)
         part = red // nbr_devs
-        inv_out[b] = y_buf[pl.ds(pl.multiple_of(q * part, 8), part)]
+        for n, b in enumerate(bs):
+            own[b] = owned[n]
+            fac_hi[b] = jnp.concatenate([lf[n][0], rt[n][0], ys[n][0]], 0)
+            fac_lo[b] = jnp.concatenate([lf[n][1], rt[n][1], ys[n][1]], 0)
+            y_buf[n] = y[n]
+        for n, b in enumerate(bs):
+            inv_out[b] = y_buf[n, pl.ds(pl.multiple_of(q * part, 8), part)]
 
     def done_sends(step, carry):
         b = box_at(step)
@@ -212,35 +216,38 @@
 
     mask_lane = lax.broadcasted_iota(jnp.int32, (1, boxes), 1)
 
-    def slot_step(step):
-        b = box_at(step)
-        pieces = []
-        for s in range(slots):
-            band_near(b, s, 0).wait()
-            c = source_of(b, s)
-            far = is_far(b, s).astype(jnp.int32)
-            weight = far * mask_far[s : s + 1, :] + (1 - far) * mask_ref[s : s + 1, :]
-            weight = jnp.sum(
-                jnp.where(mask_lane == c, weight.astype(jnp.float32), 0.0), axis=1, keepdims=True)
-            pieces += [bands[b, s, 1] * weight, bands[b, s, 0] * weight]
-        b_hi, b_lo = split(jnp.concatenate(pieces, 0))
-        dh, dl = d_hi[b], d_lo[b]
-        turned = dot(dh, b_hi, NT) + dot(dh, b_lo, NT)
-        skel_part = turned[:skel]
-        red_part = turned[skel:] + dot(dl, b_hi, NT)
-        f = dot3((fac_hi[b], fac_lo[b]), split(red_part))
-        coupled = skel_part - jnp.where(half, f[:skel], f[skel : 2 * skel])
-        flipped = red_part.T
-        z = split(f[2 * skel :])
-        near_red = split(jnp.concatenate(
-            [flipped[(2 * s + 1) * skel : (2 * s + 2) * skel] for s in range(slots)], 0))
-        u = dot3(near_red, z)
-        for s in range(slots):
-            coup_out[b, s] = coupled[:, 2 * s * skel : 2 * (s + 1) * skel]
-            one = u[s * skel : (s + 1) * skel, 2 * s * skel : (2 * s + 1) * skel]
-            packed = jnp.concatenate([one[: skel // 2], one[skel // 2 :]], 1)
-            at = b - offset_of(s) + REACH
-            sums[at] = sums[at] + packed
+    def slot_step(bs):
+        stacked = []
+        for b in bs:
+            pieces = []
+            for s in range(slots):
+                band_near(b, s, 0).wait()
+                c = source_of(b, s)
+                far = is_far(b, s).astype(jnp.int32)
+                weight = far * mask_far[s : s + 1, :] + (1 - far) * mask_ref[s : s + 1, :]
+                weight = jnp.sum(
+                    jnp.where(mask_lane == c, weight.astype(jnp.float32), 0.0),
+                    axis=1, keepdims=True)
+                pieces += [bands[b, s, 1] * weight, bands[b, s, 0] * weight]
+            stacked.append(split(jnp.concatenate(pieces, 0)))
+        dh = [d_hi[b] for b in bs]
+        dl = [d_lo[b] for b in bs]
+        turned = each(lambda d, p: dot(d, p[0], NT) + dot(d, p[1], NT), dh, stacked)
+        red_part = each(lambda t, d, p: t[skel:] + dot(d, p[0], NT), turned, dl, stacked)
+        reds = each(split, red_part)
+        f = each(lambda b, r: dot3((fac_hi[b], fac_lo[b]), r), bs, reds)
+        near_red = each(lambda r: split(jnp.concatenate(
+            [r[:, (2 * s + 1) * skel : (2 * s + 2) * skel] for s in range(slots)], 1).T), red_part)
+        zs = each(lambda a: split(a[2 * skel :]), f)
+        u = each(dot3, near_red, zs)
+        for n, b in enumerate(bs):
+            coupled = turned[n][:skel] - jnp.where(half, f[n][:skel], f[n][skel : 2 * skel])
+            for s in range(slots):
+                coup_out[b, s] = coupled[:, 2 * s * skel : 2 * (s + 1) * skel]
+                one = u[n][s * skel : (s + 1) * skel, 2 * s * skel : (2 * s + 1) * skel]
+                packed = jnp.concatenate([one[: skel // 2], one[skel // 2 :]], 1)
+                at = b - offset_of(s) + REACH
+                sums[at] = sums[at] + packed
 
     leaving = jnp.where(first_half, boxes + REACH, 0)
     landing = jnp.where(first_half, REACH, boxes)
@@ -255,48 +262,46 @@
     def ready_at(c):
         seen = jnp.where(first_half, c, boxes - 1 - c)
         last = boxes - 1 - jnp.maximum(seen - longest, 0)
-        last = jnp.where(seen >= shortest, jnp.maximum(last, REACH), REACH)
-        return jnp.where(seen < REACH, jnp.maximum(last, boxes - 2), last)
+        last = jnp.where(seen >= shortest, last, 0)
+        return jnp.where(seen < REACH, jnp.maximum(last, boxes - 3), last) // 2
 
     def sum_copy(k, c):
         return pltpu.make_async_remote_copy(
             src_ref=sums.at[c + REACH], dst_ref=others.at[k, c], send_sem=n_send.at[k, c],
             recv_sem=n_recv.at[k, c], device_id=(place, peers[k]), device_id_type=MESH)
 
-    def main(step, carry):
-        factor(step)
-
-        @pl.when(step == 0)
+    def main(trip, carry):
+        bs = [box_at(2 * trip), box_at(2 * trip + 1)]
+        factor(bs)
+
+        @pl.when(trip == 0)
         def _():
-            forward(box_at(1))
             mask_copy.wait()
 
-        slot_step(step)
-
-        @pl.when(step + 2 < boxes)
+        @pl.when(trip + 1 < boxes // 2)
         def _():
-            forward(box_at(step + 2))
-
-        @pl.when(step == REACH)
+            forward(box_at(2 * trip + 2))
+            forward(box_at(2 * trip + 3))
+
+        slot_step(bs)
+
+        @pl.when(trip == REACH // 2 - 1)
         def _():
             u_copy.start()
 
-        @pl.when(step == boxes - 2)
+        @pl.when(trip == (boxes - 3) // 2)
         def _():
             u_copy.wait()
             sums[pl.ds(landing, REACH)] = sums[pl.ds(landing, REACH)] + arrived[...]
 
         def share(c, carry):
-            @pl.when(ready_at(c) == step)
+            @pl.when(ready_at(c) == trip)
             def _():
                 for k in range(len(peers)):
                     sum_copy(k, c).start()
             return carry
 
-        @pl.when(step >= REACH)
-        def _():
-            lax.fori_loop(0, boxes, share, 0)
-
+        lax.fori_loop(0, boxes, share, 0)
         return carry
 
     early = 3
@@ -307,7 +312,8 @@
     lax.fori_loop(0, boxes, start_far, 0)
     lax.fori_loop(early, boxes, prepare, 0)
     forward(box_at(0))
-    lax.fori_loop(0, boxes, main, 0)
+    forward(box_at(1))
+    lax.fori_loop(0, boxes // 2, main, 0)
     lax.fori_loop(0, boxes, done_sends, 0)
 
     def band_done(step, carry):
@@ -375,7 +381,7 @@
             pltpu.VMEM((boxes, pts, pts), f32),
             pltpu.VMEM((boxes, slots, 2, skel, pts), f32),
             pltpu.VMEM(pair_mask.shape[::-1], jnp.int32),
-            pltpu.VMEM((red, red), f32),
+            pltpu.VMEM((2, red, red), f32),
             pltpu.VMEM((boxes, pts, pts), bf16),
             pltpu.VMEM((boxes, red, pts), bf16),
             pltpu.VMEM((boxes, 2 * skel + red, red), bf16),

time: 51 us -> 43.8 us (0.86)
  Pallas kernels: 47.6 us -> 40.4 us
    pallas_call x1, Pallas kernels: 46.6 us -> 39.4 us  [body(): pl.pallas_call(functools.partial(kernel, box_devs, nbr_devs, skel), out_s...]
where the time goes in v3:
time: 43.8 us; the launch traced here: 43.5 us
  Pallas kernels  40.4 us (92%)
  local copies, waits for them, and re-layouts  2.41 us (6%)
  between operations  0.65 us (1%)
    pallas_call x1, Pallas kernels, body(): pl.pallas_call(functools.partial(kernel, box_devs, nbr_devs, skel), out_s...  39.4 us
    unnamed x6, local copies, waits for them, and re-layouts  2.41 us
    pallas_call x1, Pallas kernels, deliver(): pl.pallas_call(functools.partial(deliver_kernel, len(arrays)), out_shape=...  1.04 us

profile of v3, /device:TPU:0, one launch (start us, length us, event | category | flops | bytes accessed | tf_op | source)
XLA Modules:
  0.0 43.5 jit_solution(2948719713584088601)
XLA Ops:
  0.6 0.0 copy-start
  0.6 1.0 %copy-done = f32[8,64,256]{2,1,0:T(8,128)S(1)} copy-done((f32[8,64,256]{2,1,0:T(8,128)S(1)}, f32[8,64,256]{2,1,0:T(8,128)}, u32[]{:S(2)}) %copy-start) | copy-done | bytes 524312
  1.7 0.0 copy-start.1
  1.7 0.7 %copy-done.1 = s32[8,256]{1,0:T(8,128)S(1)} copy-done((s32[8,256]{1,0:T(8,128)S(1)}, s32[8,256]{1,0:T(8,128)}, u32[]{:S(2)}) %copy-start.1) | copy-done | bytes 8216
  2.4 0.0 copy-start.2
  2.4 0.7 %copy-done.2 = s32[8,2]{0,1:T(2,128)S(1)} copy-done((s32[8,2]{0,1:T(2,128)S(1)}, s32[8,2]{0,1:T(2,128)}, u32[]{:S(2)}) %copy-start.2) | copy-done | bytes 88
  3.1 39.4 %level.1 = (f32[8,64,64]{2,1,0:T(8,128)S(1)}, f32[8,48,192]{2,1,0:T(8,128)S(1)}, f32[8,2,64,128]{3,2,1,0:T(8,128)S(1)}) custom-call(f32[8,64,256]{2,1,0:T(8,128)S(1)} %copy-done, s32[8,256]{1,0:T(8,128)S(1)} %copy-done.1, f32[8,64,192]{2,1,0:T(8,128)} %interp_ref.1, f32[8,2,2,64,256]{4,3,2,1,0:T(8,128)} %band_ref.1, s32[2,8]{1,0:T(2,128)S(1)} %bitcast.1), custom_call_target="tpu_custom_call" | custom-call | tf_op jit(solution)/shard_map/level/pallas_call | solution.py:371
  42.5 1.0 %deliver.1 = (f32[8,64,64]{2,1,0:T(8,128)}, f32[8,48,192]{2,1,0:T(8,128)}, f32[8,2,64,128]{3,2,1,0:T(8,128)}) custom-call(f32[8,64,64]{2,1,0:T(8,128)S(1)} %get-tuple-element.6.refs_0_, f32[8,48,192]{2,1,0:T(8,128)S(1)} %get-tuple-element.7.refs_1_, f32[8,2,64,128]{3,2,1,0:T(8,128)S(1)} %get-tuple-element.8.refs_2_), custom_call_target="tpu_custom_call" | custom-call | tf_op jit(solution)/shard_map/deliver/pallas_call | solution.py:352
Async XLA Ops:
  0.6 1.0 %copy-start = (f32[8,64,256]{2,1,0:T(8,128)S(1)}, f32[8,64,256]{2,1,0:T(8,128)}, u32[]{:S(2)}) copy-start(f32[8,64,256]{2,1,0:T(8,128)} %self_ref.1) | copy-start | bytes 1572868
  1.7 0.7 %copy-start.1 = (s32[8,256]{1,0:T(8,128)S(1)}, s32[8,256]{1,0:T(8,128)}, u32[]{:S(2)}) copy-start(s32[8,256]{1,0:T(8,128)} %order_ref.1) | copy-start | bytes 24580
  2.4 0.7 %copy-start.2 = (s32[8,2]{0,1:T(2,128)S(1)}, s32[8,2]{0,1:T(2,128)}, u32[]{:S(2)}) copy-start(s32[8,2]{0,1:T(2,128)} %param.9) | copy-start | bytes 196

commit v4 on v3

--- a/solution.py
+++ b/solution.py
@@ -403,7 +403,9 @@
         compiler_params=pltpu.CompilerParams(
             collective_id=0, has_side_effects=True, vmem_limit_bytes=52 * 1024 * 1024),
         name="level",
-    )(self_block, ordering, interp, near_band, pair_mask.T)
+    )(*[
+        pltpu.with_memory_space_constraint(a, pltpu.HBM)
+        for a in (self_block, ordering, interp, near_band, pair_mask.T)])
     return deliver(results)
 
 

time: 43.8 us -> 40.5 us (0.925)
  local copies, waits for them, and re-layouts: 2.41 us -> 0 us
  Pallas kernels: 40.4 us -> 39.7 us
    unnamed x6 -> x0, local copies, waits for them, and re-layouts: 2.41 us -> none
    pallas_call x1, Pallas kernels: 39.4 us -> 38.6 us  [body(): pl.pallas_call(functools.partial(kernel, box_devs, nbr_devs, skel), out_s...]
where the time goes in v4:
time: 40.5 us; the launch traced here: 40.3 us
  Pallas kernels  39.7 us (98%)
  between operations  0.64 us (2%)
    pallas_call x1, Pallas kernels, body(): pl.pallas_call(functools.partial(kernel, box_devs, nbr_devs, skel), out_s...  38.6 us
    pallas_call x1, Pallas kernels, deliver(): pl.pallas_call(functools.partial(deliver_kernel, len(arrays)), out_shape=...  1.04 us

profile of v4, /device:TPU:0, one launch (start us, length us, event | category | flops | bytes accessed | tf_op | source)
XLA Modules:
  0.0 40.3 jit_solution(7010573402484255984)
XLA Ops:
  0.6 38.6 %level.1 = (f32[8,64,64]{2,1,0:T(8,128)S(1)}, f32[8,48,192]{2,1,0:T(8,128)S(1)}, f32[8,2,64,128]{3,2,1,0:T(8,128)S(1)}) custom-call(f32[8,64,256]{2,1,0:T(8,128)} %self_ref.1, s32[8,256]{1,0:T(8,128)} %order_ref.1, f32[8,64,192]{2,1,0:T(8,128)} %interp_ref.1, f32[8,2,2,64,256]{4,3,2,1,0:T(8,128)} %band_ref.1, s32[2,8]{1,0:T(2,128)} %bitcast.1), custom_call_target="tpu_custom_call" | custom-call | tf_op jit(solution)/shard_map/level/pallas_call | solution.py:371
  39.3 1.0 %deliver.1 = (f32[8,64,64]{2,1,0:T(8,128)}, f32[8,48,192]{2,1,0:T(8,128)}, f32[8,2,64,128]{3,2,1,0:T(8,128)}) custom-call(f32[8,64,64]{2,1,0:T(8,128)S(1)} %get-tuple-element.6.refs_0_, f32[8,48,192]{2,1,0:T(8,128)S(1)} %get-tuple-element.7.refs_1_, f32[8,2,64,128]{3,2,1,0:T(8,128)S(1)} %get-tuple-element.8.refs_2_), custom_call_target="tpu_custom_call" | custom-call | tf_op jit(solution)/shard_map/deliver/pallas_call | solution.py:352
